TPU v7x, 128 devices: a whole 4x4x4 slice. The times are simulated.
128 devices in a mesh: row: 16 (over x_hi, z, core), col: 8 (over x_lo, y).
Axes of the slice: x: 4 (x_hi: 2, x_lo: 2; x = x_hi * 2 + x_lo), y: 4, z: 4, core: 2. Of those that a mesh axis runs over, the one named last changes fastest.
Arguments:
- a_blocks: bfloat16 [16, 8, 32, 128, 128], P('row', 'col'), may hold values from -0.5 to 0.5
- b_blocks: bfloat16 [16, 8, 128, 128, 128], P('row', 'col'), may hold values from -1.5 to 1.5
- pairs: int32 [16, 8, 4, 3, 256], P('row', 'col'), may hold values from 0 to 127, as said below
Outputs:
- c_blocks: float32 [16, 8, 64, 128, 128], P('row', 'col')
Inputs may be any that keep to these rules, and one draw needn't show every extreme that they name: `pairs`: rows 0 and 1 are slots of the left and right stacks; row 2 is a target block below 64, or 64 for a padded slot. Padded slots come after all live ones in each list. In every step some grid position has all 256 slots live and another has 64 live.
All inputs are finite; a program needn't handle non-finite values.
Results may differ from a plain program's by a relative error of at most 0.0003.
Values may be sent and summed in bfloat16 or wider, within the bound.
A program may use at most 128 MiB of HBM per device.

v0:
```python
import jax
import jax.numpy as jnp
from jax import lax
from jax.experimental import pallas as pl
from jax.experimental.pallas import tpu as pltpu
from jax.sharding import PartitionSpec as P

BS = 128
SA = 32
SB = 128
NP = 256
CBLK = 64
STEPS = 4
UNROLL = 16
NC = 4
PER = CBLK // NC
CODED_ROWS = PER * BS + PER
NB = 4
BPER = SB // NB
NONE = NP
MESH = pl.DeviceIdType.MESH


def encode(value):
    top = jnp.max(jnp.abs(value), axis=0, keepdims=True)
    exponent = jnp.ceil(jnp.log2(jnp.maximum(top, 1e-30)) + 2e-4) - 15.0
    coded = jnp.round(value * jnp.exp2(-exponent)).astype(jnp.int32).astype(jnp.int16)
    return coded, exponent


def kernel(
    tables,
    a_hbm,
    b_hbm,
    out,
    a_one,
    a_two,
    a_even,
    a_odd,
    a_own,
    b_own,
    b_prev,
    b_mate,
    t_got,
    tab,
    tab_next,
    sums,
    acc,
    part,
    code_one,
    code_zero,
    code_in,
    a_recv,
    a_send,
    t_recv,
    t_send,
    mate_recv,
    mate_send,
    b_recv,
    b_send,
    c_recv,
    zero_send,
    one_send,
    local,
    smem_sem,
    out_sem,
):
    n_row, n_col = lax.axis_size("row"), lax.axis_size("col")
    row, col = lax.axis_index("row"), lax.axis_index("col")
    odd = lax.rem(row, 2)

    def at(rows, cols):
        return (lax.rem(row + rows + n_row, n_row), lax.rem(col + cols + n_col, n_col))

    def remote(src, dst, send, recv, to):
        return pltpu.make_async_remote_copy(
            src_ref=src, dst_ref=dst, send_sem=send, recv_sem=recv, device_id=to, device_id_type=MESH
        )

    def products(a, b, tab_ref, j):
        def group(g, carry):
            for u in range(UNROLL):
                n = g * UNROLL + u
                product = jnp.dot(
                    a[tab_ref[j, 0, n]], b[tab_ref[j, 1, n]], preferred_element_type=jnp.float32
                )
                sums[n] = sums[tab_ref[j, 2, n]] + product
            return carry

        lax.fori_loop(0, NP // UNROLL, group, 0)

    def collect(dst, tab_ref, j, add):
        def some(g, carry):
            for u in range(8):
                c = g * 8 + u
                value = sums[tab_ref[j, 3, c]]
                dst[c] = dst[c] + value if add else value
            return carry

        lax.fori_loop(0, CBLK // 8, some, 0)

    def encode_chunk(k, block_of, code):
        exponents = []
        for u in range(PER):
            coded, exponent = encode(block_of(k * PER + u))
            code[k, pl.ds(u * BS, BS), :] = coded
            exponents.append(exponent)
        rows = jnp.concatenate(exponents, axis=0).astype(jnp.int32).astype(jnp.int16)
        code[k, pl.ds(PER * BS, PER), :] = rows

    def a_copy(dst, slot, index, to):
        return remote(a_hbm, dst, a_send.at[slot], a_recv.at[index], to)

    def b_chunk(ref, k):
        return ref.at[pl.ds(k * BPER, BPER)]

    def bring(src, dst, k):
        copy = pltpu.make_async_copy(src, dst, local.at[k])
        copy.start()
        return copy

    def finish():
        def chunk(k, carry):
            remote(code_in.at[k], code_in.at[k], zero_send.at[k], c_recv.at[k], at(1, 0)).wait_recv()
            rows = code_in[k, pl.ds(PER * BS, PER), :].astype(jnp.int32).astype(jnp.float32)
            for u in range(PER):
                c = k * PER + u
                coded = code_in[k, pl.ds(u * BS, BS), :].astype(jnp.int32).astype(jnp.float32)
                acc[c] = acc[c] + coded * jnp.exp2(rows[u : u + 1])
            span = pl.ds(k * PER, PER)
            pltpu.make_async_copy(acc.at[span], out.at[span], out_sem.at[k]).start()
            return carry

        lax.fori_loop(0, NC, chunk, 0)

        def drained(k, carry):
            span = pl.ds(k * PER, PER)
            pltpu.make_async_copy(acc.at[span], out.at[span], out_sem.at[k]).wait()
            return carry

        lax.fori_loop(0, NC, drained, 0)

    barrier = pltpu.get_barrier_semaphore()

    def greet(sources, targets):
        for to in sources:
            pl.semaphore_signal(barrier, inc=1, device_id=at(*to), device_id_type=MESH)
        pl.semaphore_wait(barrier, targets)

    @pl.when(odd == 0)
    def _():
        greet([(0, -1), (2, -2), (2, -3), (3, -3), (2, 0), (3, 0), (-1, 0), (-2, 0)], 7)

    @pl.when(odd == 1)
    def _():
        greet([(0, -1), (0, -2), (-1, 0), (-3, 0)], 5)

    @pl.when(odd == 0)
    def _():
        left = a_copy(a_one, 0, 0, at(0, 1))
        left.start()
        listed = remote(
            tables.at[pl.ds(2, 2)], t_got.at[pl.ds(0, 2)], t_send.at[0], t_recv.at[0], at(-2, 0)
        )
        listed.start()
        mate = remote(b_hbm, b_mate, mate_send.at[0], mate_recv.at[0], at(1, 0))
        mate.start()
        own_tab = bring(tables, tab, 0)
        own_a = bring(a_hbm, a_own, 1)
        own_b = bring(b_hbm, b_own, 2)
        sums[NONE] = jnp.zeros((BS, BS), jnp.float32)
        own_tab.wait()
        own_a.wait()
        own_b.wait()
        products(a_own, b_own, tab, 0)
        collect(acc, tab, 0, False)
        listed.wait_recv()
        remote(
            tables.at[pl.ds(3, 1)], t_got.at[pl.ds(2, 1)], t_send.at[0], t_recv.at[1], at(1, 0)
        ).wait_recv()
        got = pltpu.make_async_copy(t_got, tab_next, smem_sem.at[0])
        got.start()
        left.wait_send()
        far = a_copy(a_even, 1, 2, at(-2, 3))
        far.start()
        got.wait()
        a_copy(a_odd, 2, 3, at(1, 0)).wait_recv()
        products(a_odd, b_own, tab_next, 2)

        def one(k, carry):
            encode_chunk(k, lambda c: sums[tab_next[2, 3, c]], code_one)
            return carry

        lax.fori_loop(0, NC, one, 0)
        far.wait_send()
        two = a_copy(a_two, 2, 1, at(-2, 2))
        two.start()
        two.wait_recv()
        products(a_two, b_own, tab_next, 0)
        collect(part, tab_next, 0, False)

        def pass_on(k, carry):
            copy = remote(
                b_chunk(b_prev, k), b_chunk(b_prev, k), b_send.at[k], b_recv.at[k], at(1, 0)
            )
            copy.wait_recv()
            copy.start()
            return carry

        lax.fori_loop(0, NB, pass_on, 0)

        def send_one(k, carry):
            remote(code_one.at[k], code_in.at[k], one_send.at[k], c_recv.at[k], at(3, 0)).start()
            return carry

        lax.fori_loop(0, NC, send_one, 0)
        far.wait_recv()
        products(a_even, b_prev, tab_next, 1)

        def zero(k, carry):
            encode_chunk(k, lambda c: part[c] + sums[tab_next[1, 3, c]], code_zero)
            remote(code_zero.at[k], code_in.at[k], zero_send.at[k], c_recv.at[k], at(2, 0)).start()
            return carry

        lax.fori_loop(0, NC, zero, 0)
        left.wait_recv()
        products(a_one, b_prev, tab, 1)
        collect(acc, tab, 1, True)
        two.wait_send()
        listed.wait_send()
        mate.wait_send()
        finish()

        def drained(k, carry):
            remote(
                b_chunk(b_prev, k), b_chunk(b_prev, k), b_send.at[k], b_recv.at[k], at(1, 0)
            ).wait_send()
            return carry

        lax.fori_loop(0, NB, drained, 0)

        def gone(k, carry):
            remote(code_one.at[k], code_in.at[k], one_send.at[k], c_recv.at[k], at(3, 0)).wait_send()
            remote(code_zero.at[k], code_in.at[k], zero_send.at[k], c_recv.at[k], at(2, 0)).wait_send()
            return carry

        lax.fori_loop(0, NC, gone, 0)

    @pl.when(odd == 1)
    def _():
        def give(k, carry):
            remote(
                b_chunk(b_hbm, k), b_chunk(b_prev, k), b_send.at[k], b_recv.at[k], at(1, 0)
            ).start()
            return carry

        lax.fori_loop(0, NB, give, 0)
        far = a_copy(a_odd, 0, 3, at(-3, 3))
        far.start()
        listed = remote(
            tables.at[pl.ds(3, 1)], t_got.at[pl.ds(2, 1)], t_send.at[0], t_recv.at[1], at(-3, 0)
        )
        listed.start()
        own_tab = bring(tables, tab, 0)
        own_a = bring(a_hbm, a_own, 1)
        own_b = bring(b_hbm, b_own, 2)
        sums[NONE] = jnp.zeros((BS, BS), jnp.float32)
        own_tab.wait()
        own_a.wait()
        own_b.wait()
        products(a_own, b_own, tab, 0)
        collect(acc, tab, 0, False)
        far.wait_send()
        left = a_copy(a_one, 1, 0, at(0, 1))
        left.start()
        remote(b_hbm, b_mate, mate_send.at[0], mate_recv.at[0], at(-1, 0)).wait_recv()
        left.wait_recv()
        products(a_one, b_mate, tab, 1)
        collect(acc, tab, 1, True)
        left.wait_send()
        two = a_copy(a_two, 2, 1, at(0, 2))
        two.start()
        two.wait_recv()

        def arrived(k, carry):
            remote(
                b_chunk(b_prev, k), b_chunk(b_prev, k), b_send.at[k], b_recv.at[k], at(1, 0)
            ).wait_recv()
            return carry

        lax.fori_loop(0, NB, arrived, 0)
        products(a_two, b_prev, tab, 2)
        collect(acc, tab, 2, True)
        two.wait_send()
        listed.wait_send()

        def drained(k, carry):
            remote(
                b_chunk(b_hbm, k), b_chunk(b_prev, k), b_send.at[k], b_recv.at[k], at(1, 0)
            ).wait_send()
            return carry

        lax.fori_loop(0, NB, drained, 0)
        finish()


def grid_product(tables, a, b):
    anywhere = pl.BlockSpec(memory_space=pl.ANY)
    left = pltpu.VMEM((SA, BS, BS), jnp.bfloat16)
    right = pltpu.VMEM((SB, BS, BS), jnp.bfloat16)
    code = pltpu.VMEM((NC, CODED_ROWS, BS), jnp.int16)
    dma = pltpu.SemaphoreType.DMA
    return pl.pallas_call(
        kernel,
        out_shape=jax.ShapeDtypeStruct((CBLK, BS, BS), jnp.float32),
        in_specs=[anywhere] * 3,
        out_specs=anywhere,
        scratch_shapes=[left] * 5
        + [right] * 3
        + [
            pltpu.VMEM((3, 4, NP), jnp.int32),
            pltpu.SMEM((STEPS, 4, NP), jnp.int32),
            pltpu.SMEM((3, 4, NP), jnp.int32),
            pltpu.VMEM((NP + 1, BS, BS), jnp.float32),
            pltpu.VMEM((CBLK, BS, BS), jnp.float32),
            pltpu.VMEM((CBLK, BS, BS), jnp.float32),
        ]
        + [code] * 3
        + [
            dma((4,)),
            dma((3,)),
            dma((2,)),
            dma((1,)),
            dma((1,)),
            dma((1,)),
            dma((NB,)),
            dma((NB,)),
            dma((NC,)),
            dma((NC,)),
            dma((NC,)),
            dma((3,)),
            dma((1,)),
            dma((NC,)),
        ],
        compiler_params=pltpu.CompilerParams(
            collective_id=0, has_side_effects=True, vmem_limit_bytes=58 << 20
        ),
        cost_estimate=pl.CostEstimate(
            flops=2 * STEPS * NP * BS**3, bytes_accessed=32 << 20, transcendentals=0
        ),
    )(tables, a, b)


def listed(pairs):
    target = pairs[:, 2, :]
    slot = jnp.arange(NP, dtype=jnp.int32)
    same = (target[:, :, None] == target[:, None, :]) & (slot[:, None] < slot[None, :])
    before = jnp.max(jnp.where(same, slot[:, None], -1), axis=1)
    hit = target[:, :, None] == slot[None, None, :]
    final = jnp.max(jnp.where(hit, slot[:, None], -1), axis=1)
    found = jnp.stack([before, final], axis=1)
    found = jnp.where(found < 0, NONE, found)
    return jnp.concatenate([pairs[:, :2, :], found], axis=1)


def on_device(a_blocks, b_blocks, pairs):
    return grid_product(listed(pairs[0, 0]), a_blocks[0, 0], b_blocks[0, 0])[None, None]


def solution(mesh):
    spec = P("row", "col", None, None, None)
    return jax.shard_map(
        on_device, mesh=mesh, in_specs=(spec,) * 3, out_specs=spec, check_vma=False
    )
```

profile of v0, /device:TPU:64, one launch (start us, length us, event | category | flops | bytes accessed | tf_op | source)
XLA Modules:
  0.0 198.4 jit_solution(2792590125994910369)
XLA Ops:
  0.0 0.7 copy.9
  0.8 0.5 select_reduce_fusion.1
  1.3 0.6 pad_add_fusion.tables
  2.0 191.8 %shard_map.37 = f32[64,128,128]{2,1,0:T(8,128)} custom-call(s32[4,4,256]{2,1,0:T(4,128)} %pad_add_fusion.tables, bf16[32,128,128]{2,1,0:T(8,128)(2,1)} %bitcast.14, bf16[128,128,128]{2,1,0:T(8,128)(2,1)} %bitcast.13), custom_call_target="tpu_custom_call" | custom-call | flops 4294967296 | bytes 33554432 | tf_op jit(solution)/shard_map/pallas_call | solution.py:313
  193.7 4.7 %copy.12 = f32[1,1,64,128,128]{4,3,2,1,0:T(8,128)} copy(f32[1,1,64,128,128]{4,3,2,1,0:T(8,128)} %bitcast.9) | data formatting | bytes 8388608
  (7 shorter events, 0.1 us)
where the time goes:
time: 199 us; the launch traced here: 198 us
  Pallas kernels  192 us (96%)
  local copies, waits for them, and re-layouts  5.43 us (3%)
    pallas_call x1, Pallas kernels, grid_product(): pl.pallas_call(kernel, out_shape=jax.ShapeDtypeStruct((CBLK, BS, BS), jnp...  192 us
    unnamed x3, local copies, waits for them, and re-layouts  5.41 us

commit v1 on v0

--- a/solution.py
+++ b/solution.py
@@ -17,6 +17,8 @@
 CODED_ROWS = PER * BS + PER
 NB = 4
 BPER = SB // NB
+RELAYED = (3,)
+DIRECT = tuple(k for k in range(NB) if k not in RELAYED)
 NONE = NP
 MESH = pl.DeviceIdType.MESH
 
@@ -38,6 +40,7 @@
     a_even,
     a_odd,
     a_own,
+    a_flip,
     b_own,
     b_prev,
     b_mate,
@@ -58,6 +61,8 @@
     mate_send,
     b_recv,
     b_send,
+    hub_recv,
+    hub_send,
     c_recv,
     zero_send,
     one_send,
@@ -108,8 +113,24 @@
         rows = jnp.concatenate(exponents, axis=0).astype(jnp.int32).astype(jnp.int16)
         code[k, pl.ds(PER * BS, PER), :] = rows
 
-    def a_copy(dst, slot, index, to):
-        return remote(a_hbm, dst, a_send.at[slot], a_recv.at[index], to)
+    lane = lax.rem(col, n_col // 2)
+    plane = col - lane
+
+    def along(rows, steps):
+        half = n_col // 2
+        return (lax.rem(row + rows + n_row, n_row), plane + lax.rem(lane + steps + half, half))
+
+    def a_copy(dst, slot, index, to, src=None):
+        return remote(a_hbm if src is None else src, dst, a_send.at[slot], a_recv.at[index], to)
+
+    def a_start(dst, slot, index, to, steps):
+        @pl.when(lane + steps < n_col // 2)
+        def _():
+            a_copy(dst, slot, index, to).start()
+
+        @pl.when(lane + steps >= n_col // 2)
+        def _():
+            a_copy(dst, slot, index, to, a_flip).start()
 
     def b_chunk(ref, k):
         return ref.at[pl.ds(k * BPER, BPER)]
@@ -141,24 +162,50 @@
         lax.fori_loop(0, NC, drained, 0)
 
     barrier = pltpu.get_barrier_semaphore()
-
-    def greet(sources, targets):
-        for to in sources:
-            pl.semaphore_signal(barrier, inc=1, device_id=at(*to), device_id_type=MESH)
-        pl.semaphore_wait(barrier, targets)
+    place = lax.rem(row, n_row // 2)
+    at_start = place == 0
+    hub = place == 1
+    seam = place == n_row // 2 - 1
+    across = n_row // 2
+
+    def hail(to):
+        pl.semaphore_signal(barrier, inc=1, device_id=to, device_id_type=MESH)
 
     @pl.when(odd == 0)
     def _():
-        greet([(0, -1), (2, -2), (2, -3), (3, -3), (2, 0), (3, 0), (-1, 0), (-2, 0)], 7)
+        for rows, steps in ((0, -1), (2, -2), (2, -3), (3, -3)):
+            hail(along(rows, steps))
+        for rows, cols in ((0, n_col // 2), (2, 0), (3, 0), (-1, 0), (-2, 0)):
+            hail(at(rows, cols))
+
+        @pl.when(at_start)
+        def _():
+            hail(at(across + 1, 0))
+
+        pl.semaphore_wait(barrier, 8)
 
     @pl.when(odd == 1)
     def _():
-        greet([(0, -1), (0, -2), (-1, 0), (-3, 0)], 5)
+        for rows, steps in ((0, -1), (0, -2)):
+            hail(along(rows, steps))
+        for rows, cols in ((0, n_col // 2), (-1, 0), (-3, 0)):
+            hail(at(rows, cols))
+
+        @pl.when(hub)
+        def _():
+            hail(at(across - 2, 0))
+
+        pl.semaphore_wait(barrier, 6 + jnp.where(hub | seam, 1, 0))
+
+    flip = a_copy(a_flip, 3, 4, at(0, n_col // 2))
+    flip.start()
 
     @pl.when(odd == 0)
     def _():
-        left = a_copy(a_one, 0, 0, at(0, 1))
-        left.start()
+        @pl.when(lane + 1 < n_col // 2)
+        def _():
+            a_copy(a_one, 0, 0, along(0, 1)).start()
+
         listed = remote(
             tables.at[pl.ds(2, 2)], t_got.at[pl.ds(0, 2)], t_send.at[0], t_recv.at[0], at(-2, 0)
         )
@@ -174,16 +221,25 @@
         own_b.wait()
         products(a_own, b_own, tab, 0)
         collect(acc, tab, 0, False)
+        flip.wait_recv()
+        left = a_copy(a_one, 0, 0, along(0, 1))
+        far = a_copy(a_even, 2, 2, along(-2, 3))
+        two = a_copy(a_two, 1, 1, along(-2, 2))
+        a_start(a_even, 2, 2, along(-2, 3), 3)
+
+        @pl.when(lane + 1 >= n_col // 2)
+        def _():
+            a_copy(a_one, 0, 0, along(0, 1), a_flip).start()
+
         listed.wait_recv()
         remote(
             tables.at[pl.ds(3, 1)], t_got.at[pl.ds(2, 1)], t_send.at[0], t_recv.at[1], at(1, 0)
         ).wait_recv()
         got = pltpu.make_async_copy(t_got, tab_next, smem_sem.at[0])
         got.start()
-        left.wait_send()
-        far = a_copy(a_even, 1, 2, at(-2, 3))
-        far.start()
         got.wait()
+        far.wait_send()
+        a_start(a_two, 1, 1, along(-2, 2), 2)
         a_copy(a_odd, 2, 3, at(1, 0)).wait_recv()
         products(a_odd, b_own, tab_next, 2)
 
@@ -192,12 +248,14 @@
             return carry
 
         lax.fori_loop(0, NC, one, 0)
-        far.wait_send()
-        two = a_copy(a_two, 2, 1, at(-2, 2))
-        two.start()
-        two.wait_recv()
-        products(a_two, b_own, tab_next, 0)
-        collect(part, tab_next, 0, False)
+
+        def send_one(k, carry):
+            remote(code_one.at[k], code_in.at[k], one_send.at[k], c_recv.at[k], at(3, 0)).start()
+            return carry
+
+        @pl.when(at_start)
+        def _():
+            lax.fori_loop(0, NC, send_one, 0)
 
         def pass_on(k, carry):
             copy = remote(
@@ -209,16 +267,18 @@
 
         lax.fori_loop(0, NB, pass_on, 0)
 
-        def send_one(k, carry):
-            remote(code_one.at[k], code_in.at[k], one_send.at[k], c_recv.at[k], at(3, 0)).start()
-            return carry
-
-        lax.fori_loop(0, NC, send_one, 0)
+        @pl.when(jnp.logical_not(at_start))
+        def _():
+            lax.fori_loop(0, NC, send_one, 0)
+
         far.wait_recv()
         products(a_even, b_prev, tab_next, 1)
+        collect(part, tab_next, 1, False)
+        two.wait_recv()
+        products(a_two, b_own, tab_next, 0)
 
         def zero(k, carry):
-            encode_chunk(k, lambda c: part[c] + sums[tab_next[1, 3, c]], code_zero)
+            encode_chunk(k, lambda c: part[c] + sums[tab_next[0, 3, c]], code_zero)
             remote(code_zero.at[k], code_in.at[k], zero_send.at[k], c_recv.at[k], at(2, 0)).start()
             return carry
 
@@ -226,10 +286,11 @@
         left.wait_recv()
         products(a_one, b_prev, tab, 1)
         collect(acc, tab, 1, True)
+        left.wait_send()
         two.wait_send()
+        flip.wait_send()
         listed.wait_send()
         mate.wait_send()
-        finish()
 
         def drained(k, carry):
             remote(
@@ -238,6 +299,7 @@
             return carry
 
         lax.fori_loop(0, NB, drained, 0)
+        finish()
 
         def gone(k, carry):
             remote(code_one.at[k], code_in.at[k], one_send.at[k], c_recv.at[k], at(3, 0)).wait_send()
@@ -248,15 +310,39 @@
 
     @pl.when(odd == 1)
     def _():
-        def give(k, carry):
-            remote(
+        def b_copy(k):
+            return remote(
                 b_chunk(b_hbm, k), b_chunk(b_prev, k), b_send.at[k], b_recv.at[k], at(1, 0)
-            ).start()
-            return carry
-
-        lax.fori_loop(0, NB, give, 0)
-        far = a_copy(a_odd, 0, 3, at(-3, 3))
-        far.start()
+            )
+
+        def to_hub(k):
+            return remote(
+                b_chunk(b_hbm, k),
+                (a_even, a_odd)[k - 2],
+                b_send.at[k],
+                hub_recv.at[k - 2],
+                at(2 - across, 0),
+            )
+
+        def from_hub(k):
+            return remote(
+                (a_even, a_odd)[k - 2],
+                b_chunk(b_prev, k),
+                hub_send.at[k - 2],
+                b_recv.at[k],
+                at(across - 1, 0),
+            )
+
+        @pl.when(seam)
+        def _():
+            for k in RELAYED:
+                to_hub(k).start()
+
+        @pl.when(jnp.logical_not(seam))
+        def _():
+            for k in range(NB):
+                b_copy(k).start()
+
         listed = remote(
             tables.at[pl.ds(3, 1)], t_got.at[pl.ds(2, 1)], t_send.at[0], t_recv.at[1], at(-3, 0)
         )
@@ -264,43 +350,62 @@
         own_tab = bring(tables, tab, 0)
         own_a = bring(a_hbm, a_own, 1)
         own_b = bring(b_hbm, b_own, 2)
+
+        @pl.when(lane + 1 < n_col // 2)
+        def _():
+            a_copy(a_one, 0, 0, along(0, 1)).start()
+
         sums[NONE] = jnp.zeros((BS, BS), jnp.float32)
         own_tab.wait()
         own_a.wait()
         own_b.wait()
         products(a_own, b_own, tab, 0)
         collect(acc, tab, 0, False)
-        far.wait_send()
-        left = a_copy(a_one, 1, 0, at(0, 1))
-        left.start()
+        flip.wait_recv()
+        left = a_copy(a_one, 0, 0, along(0, 1))
+        far = a_copy(a_odd, 2, 3, along(-3, 3))
+        two = a_copy(a_two, 1, 1, along(0, 2))
+        a_start(a_odd, 2, 3, along(-3, 3), 3)
+
+        @pl.when(lane + 1 >= n_col // 2)
+        def _():
+            a_copy(a_one, 0, 0, along(0, 1), a_flip).start()
+
+        @pl.when(seam)
+        def _():
+            for k in DIRECT:
+                b_copy(k).start()
+
         remote(b_hbm, b_mate, mate_send.at[0], mate_recv.at[0], at(-1, 0)).wait_recv()
         left.wait_recv()
         products(a_one, b_mate, tab, 1)
         collect(acc, tab, 1, True)
-        left.wait_send()
-        two = a_copy(a_two, 2, 1, at(0, 2))
-        two.start()
+        far.wait_send()
+        a_start(a_two, 1, 1, along(0, 2), 2)
+
+        @pl.when(hub)
+        def _():
+            for k in RELAYED:
+                to_hub(k).wait_recv()
+                from_hub(k).start()
+
         two.wait_recv()
-
-        def arrived(k, carry):
-            remote(
-                b_chunk(b_prev, k), b_chunk(b_prev, k), b_send.at[k], b_recv.at[k], at(1, 0)
-            ).wait_recv()
-            return carry
-
-        lax.fori_loop(0, NB, arrived, 0)
+        for k in range(NB):
+            b_copy(k).wait_recv()
         products(a_two, b_prev, tab, 2)
         collect(acc, tab, 2, True)
+        left.wait_send()
         two.wait_send()
+        flip.wait_send()
         listed.wait_send()
-
-        def drained(k, carry):
-            remote(
-                b_chunk(b_hbm, k), b_chunk(b_prev, k), b_send.at[k], b_recv.at[k], at(1, 0)
-            ).wait_send()
-            return carry
-
-        lax.fori_loop(0, NB, drained, 0)
+        for k in range(NB):
+            b_copy(k).wait_send()
+
+        @pl.when(hub)
+        def _():
+            for k in RELAYED:
+                from_hub(k).wait_send()
+
         finish()
 
 
@@ -315,7 +420,7 @@
         out_shape=jax.ShapeDtypeStruct((CBLK, BS, BS), jnp.float32),
         in_specs=[anywhere] * 3,
         out_specs=anywhere,
-        scratch_shapes=[left] * 5
+        scratch_shapes=[left] * 6
         + [right] * 3
         + [
             pltpu.VMEM((3, 4, NP), jnp.int32),
@@ -327,14 +432,16 @@
         ]
         + [code] * 3
         + [
+            dma((5,)),
             dma((4,)),
-            dma((3,)),
             dma((2,)),
             dma((1,)),
             dma((1,)),
             dma((1,)),
             dma((NB,)),
             dma((NB,)),
+            dma((2,)),
+            dma((2,)),
             dma((NC,)),
             dma((NC,)),
             dma((NC,)),

time: 199 us -> 141 us (0.71)
  the two profiles are of different devices: /device:TPU:64 before, /device:TPU:0 now
where the time goes in v1:
time: 141 us; the launch traced here: 140 us
  Pallas kernels  134 us (95%)
  local copies, waits for them, and re-layouts  5.43 us (4%)
    pallas_call x1, Pallas kernels, grid_product(): pl.pallas_call(kernel, out_shape=jax.ShapeDtypeStruct((CBLK, BS, BS), jnp...  134 us
    unnamed x3, local copies, waits for them, and re-layouts  5.41 us

profile of v1, /device:TPU:0, one launch (start us, length us, event | category | flops | bytes accessed | tf_op | source)
XLA Modules:
  0.0 140.3 jit_solution(15778092109147750878)
XLA Ops:
  0.0 0.7 copy.9
  0.8 0.5 select_reduce_fusion.1
  1.3 0.6 pad_add_fusion.tables
  2.0 133.7 %shard_map.37 = f32[64,128,128]{2,1,0:T(8,128)} custom-call(s32[4,4,256]{2,1,0:T(4,128)} %pad_add_fusion.tables, bf16[32,128,128]{2,1,0:T(8,128)(2,1)} %bitcast.14, bf16[128,128,128]{2,1,0:T(8,128)(2,1)} %bitcast.13), custom_call_target="tpu_custom_call" | custom-call | flops 4294967296 | bytes 33554432 | tf_op jit(solution)/shard_map/pallas_call | solution.py:418
  135.6 4.7 %copy.12 = f32[1,1,64,128,128]{4,3,2,1,0:T(8,128)} copy(f32[1,1,64,128,128]{4,3,2,1,0:T(8,128)} %bitcast.9) | data formatting | bytes 8388608
  (7 shorter events, 0.1 us)

commit v2 on v1

--- a/solution.py
+++ b/solution.py
@@ -140,14 +140,17 @@
         copy.start()
         return copy
 
+    def absorb(k):
+        remote(code_in.at[k], code_in.at[k], zero_send.at[k], c_recv.at[k], at(1, 0)).wait_recv()
+        rows = code_in[k, pl.ds(PER * BS, PER), :].astype(jnp.int32).astype(jnp.float32)
+        for u in range(PER):
+            c = k * PER + u
+            coded = code_in[k, pl.ds(u * BS, BS), :].astype(jnp.int32).astype(jnp.float32)
+            acc[c] = acc[c] + coded * jnp.exp2(rows[u : u + 1])
+
     def finish():
         def chunk(k, carry):
-            remote(code_in.at[k], code_in.at[k], zero_send.at[k], c_recv.at[k], at(1, 0)).wait_recv()
-            rows = code_in[k, pl.ds(PER * BS, PER), :].astype(jnp.int32).astype(jnp.float32)
-            for u in range(PER):
-                c = k * PER + u
-                coded = code_in[k, pl.ds(u * BS, BS), :].astype(jnp.int32).astype(jnp.float32)
-                acc[c] = acc[c] + coded * jnp.exp2(rows[u : u + 1])
+            absorb(k)
             span = pl.ds(k * PER, PER)
             pltpu.make_async_copy(acc.at[span], out.at[span], out_sem.at[k]).start()
             return carry
@@ -227,10 +230,6 @@
         two = a_copy(a_two, 1, 1, along(-2, 2))
         a_start(a_even, 2, 2, along(-2, 3), 3)
 
-        @pl.when(lane + 1 >= n_col // 2)
-        def _():
-            a_copy(a_one, 0, 0, along(0, 1), a_flip).start()
-
         listed.wait_recv()
         remote(
             tables.at[pl.ds(3, 1)], t_got.at[pl.ds(2, 1)], t_send.at[0], t_recv.at[1], at(1, 0)
@@ -240,6 +239,7 @@
         got.wait()
         far.wait_send()
         a_start(a_two, 1, 1, along(-2, 2), 2)
+
         a_copy(a_odd, 2, 3, at(1, 0)).wait_recv()
         products(a_odd, b_own, tab_next, 2)
 
@@ -283,11 +283,16 @@
             return carry
 
         lax.fori_loop(0, NC, zero, 0)
+        two.wait_send()
+
+        @pl.when(lane + 1 >= n_col // 2)
+        def _():
+            a_copy(a_one, 0, 0, along(0, 1), a_flip).start()
+
         left.wait_recv()
         products(a_one, b_prev, tab, 1)
         collect(acc, tab, 1, True)
         left.wait_send()
-        two.wait_send()
         flip.wait_send()
         listed.wait_send()
         mate.wait_send()
@@ -367,33 +372,43 @@
         two = a_copy(a_two, 1, 1, along(0, 2))
         a_start(a_odd, 2, 3, along(-3, 3), 3)
 
-        @pl.when(lane + 1 >= n_col // 2)
-        def _():
-            a_copy(a_one, 0, 0, along(0, 1), a_flip).start()
-
         @pl.when(seam)
         def _():
             for k in DIRECT:
                 b_copy(k).start()
 
+        far.wait_send()
+
+        @pl.when(lane + 1 >= n_col // 2)
+        def _():
+            a_copy(a_one, 0, 0, along(0, 1), a_flip).start()
+        @pl.when(hub)
+        def _():
+            for k in RELAYED:
+                to_hub(k).wait_recv()
+                from_hub(k).start()
+
+        def absorb_and_send(k, carry):
+            absorb(k)
+
+            @pl.when(k == 0)
+            def _():
+                a_start(a_two, 1, 1, along(0, 2), 2)
+
+            return carry
+
+        lax.fori_loop(0, NC, absorb_and_send, 0)
         remote(b_hbm, b_mate, mate_send.at[0], mate_recv.at[0], at(-1, 0)).wait_recv()
         left.wait_recv()
         products(a_one, b_mate, tab, 1)
         collect(acc, tab, 1, True)
-        far.wait_send()
-        a_start(a_two, 1, 1, along(0, 2), 2)
-
-        @pl.when(hub)
-        def _():
-            for k in RELAYED:
-                to_hub(k).wait_recv()
-                from_hub(k).start()
-
         two.wait_recv()
         for k in range(NB):
             b_copy(k).wait_recv()
         products(a_two, b_prev, tab, 2)
         collect(acc, tab, 2, True)
+        shown = pltpu.make_async_copy(acc, out, out_sem.at[0])
+        shown.start()
         left.wait_send()
         two.wait_send()
         flip.wait_send()
@@ -406,7 +421,7 @@
             for k in RELAYED:
                 from_hub(k).wait_send()
 
-        finish()
+        shown.wait()
 
 
 def grid_product(tables, a, b):

time: 141 us -> 123 us (0.87)
  Pallas kernels: 134 us -> 116 us
    pallas_call x1, Pallas kernels: 134 us -> 116 us  [grid_product(): pl.pallas_call(kernel, out_shape=jax.ShapeDtypeStruct((CBLK, BS, BS), jnp...]
where the time goes in v2:
time: 123 us; the launch traced here: 122 us
  Pallas kernels  116 us (94%)
  local copies, waits for them, and re-layouts  5.43 us (4%)
    pallas_call x1, Pallas kernels, grid_product(): pl.pallas_call(kernel, out_shape=jax.ShapeDtypeStruct((CBLK, BS, BS), jnp...  116 us
    unnamed x3, local copies, waits for them, and re-layouts  5.41 us

profile of v2, /device:TPU:0, one launch (start us, length us, event | category | flops | bytes accessed | tf_op | source)
XLA Modules:
  0.0 122.3 jit_solution(9376284385458592422)
XLA Ops:
  0.0 0.7 copy.9
  0.8 0.5 select_reduce_fusion.1
  1.3 0.6 pad_add_fusion.tables
  2.0 115.7 %shard_map.37 = f32[64,128,128]{2,1,0:T(8,128)} custom-call(s32[4,4,256]{2,1,0:T(4,128)} %pad_add_fusion.tables, bf16[32,128,128]{2,1,0:T(8,128)(2,1)} %bitcast.14, bf16[128,128,128]{2,1,0:T(8,128)(2,1)} %bitcast.13), custom_call_target="tpu_custom_call" | custom-call | flops 4294967296 | bytes 33554432 | tf_op jit(solution)/shard_map/pallas_call | solution.py:433
  117.6 4.7 %copy.12 = f32[1,1,64,128,128]{4,3,2,1,0:T(8,128)} copy(f32[1,1,64,128,128]{4,3,2,1,0:T(8,128)} %bitcast.9) | data formatting | bytes 8388608
  (7 shorter events, 0.1 us)

commit v3 on v2

--- a/solution.py
+++ b/solution.py
@@ -34,7 +34,7 @@
     tables,
     a_hbm,
     b_hbm,
-    out,
+    acc,
     a_one,
     a_two,
     a_even,
@@ -48,7 +48,6 @@
     tab,
     tab_next,
     sums,
-    acc,
     part,
     code_one,
     code_zero,
@@ -68,7 +67,6 @@
     one_send,
     local,
     smem_sem,
-    out_sem,
 ):
     n_row, n_col = lax.axis_size("row"), lax.axis_size("col")
     row, col = lax.axis_index("row"), lax.axis_index("col")
@@ -151,18 +149,9 @@
     def finish():
         def chunk(k, carry):
             absorb(k)
-            span = pl.ds(k * PER, PER)
-            pltpu.make_async_copy(acc.at[span], out.at[span], out_sem.at[k]).start()
             return carry
 
         lax.fori_loop(0, NC, chunk, 0)
-
-        def drained(k, carry):
-            span = pl.ds(k * PER, PER)
-            pltpu.make_async_copy(acc.at[span], out.at[span], out_sem.at[k]).wait()
-            return carry
-
-        lax.fori_loop(0, NC, drained, 0)
 
     barrier = pltpu.get_barrier_semaphore()
     place = lax.rem(row, n_row // 2)
@@ -407,8 +396,6 @@
             b_copy(k).wait_recv()
         products(a_two, b_prev, tab, 2)
         collect(acc, tab, 2, True)
-        shown = pltpu.make_async_copy(acc, out, out_sem.at[0])
-        shown.start()
         left.wait_send()
         two.wait_send()
         flip.wait_send()
@@ -421,11 +408,10 @@
             for k in RELAYED:
                 from_hub(k).wait_send()
 
-        shown.wait()
-
 
 def grid_product(tables, a, b):
     anywhere = pl.BlockSpec(memory_space=pl.ANY)
+    in_hbm = pl.BlockSpec(memory_space=pltpu.HBM)
     left = pltpu.VMEM((SA, BS, BS), jnp.bfloat16)
     right = pltpu.VMEM((SB, BS, BS), jnp.bfloat16)
     code = pltpu.VMEM((NC, CODED_ROWS, BS), jnp.int16)
@@ -433,8 +419,8 @@
     return pl.pallas_call(
         kernel,
         out_shape=jax.ShapeDtypeStruct((CBLK, BS, BS), jnp.float32),
-        in_specs=[anywhere] * 3,
-        out_specs=anywhere,
+        in_specs=[anywhere, in_hbm, in_hbm],
+        out_specs=pl.BlockSpec(memory_space=pltpu.VMEM),
         scratch_shapes=[left] * 6
         + [right] * 3
         + [
@@ -442,7 +428,6 @@
             pltpu.SMEM((STEPS, 4, NP), jnp.int32),
             pltpu.SMEM((3, 4, NP), jnp.int32),
             pltpu.VMEM((NP + 1, BS, BS), jnp.float32),
-            pltpu.VMEM((CBLK, BS, BS), jnp.float32),
             pltpu.VMEM((CBLK, BS, BS), jnp.float32),
         ]
         + [code] * 3
@@ -462,10 +447,9 @@
             dma((NC,)),
             dma((3,)),
             dma((1,)),
-            dma((NC,)),
         ],
         compiler_params=pltpu.CompilerParams(
-            collective_id=0, has_side_effects=True, vmem_limit_bytes=58 << 20
+            collective_id=0, has_side_effects=True, vmem_limit_bytes=48 << 20
         ),
         cost_estimate=pl.CostEstimate(
             flops=2 * STEPS * NP * BS**3, bytes_accessed=32 << 20, transcendentals=0

time: 123 us -> 119 us (0.967)
  Pallas kernels: 116 us -> 114 us
  local copies, waits for them, and re-layouts: 5.43 us -> 3.97 us
    unnamed x3 -> x5, local copies, waits for them, and re-layouts: 5.41 us -> 3.95 us
where the time goes in v3:
time: 119 us
  Pallas kernels  114 us (96%)
  local copies, waits for them, and re-layouts  3.97 us (3%)
    pallas_call x1, Pallas kernels, grid_product(): pl.pallas_call(kernel, out_shape=jax.ShapeDtypeStruct((CBLK, BS, BS), jnp...  114 us
    unnamed x5, local copies, waits for them, and re-layouts  3.95 us

profile of v3, /device:TPU:0, one launch (start us, length us, event | category | flops | bytes accessed | tf_op | source)
XLA Modules:
  0.0 119.1 jit_solution(4575727070216388123)
XLA Ops:
  0.0 0.7 copy.9
  0.8 0.5 select_reduce_fusion.1
  1.4 0.0 copy-start
  1.4 1.2 %copy-done = bf16[1,1,32,128,128]{4,3,2,1,0:T(8,128)(2,1)S(1)} copy-done((bf16[1,1,32,128,128]{4,3,2,1,0:T(8,128)(2,1)S(1)}, bf16[1,1,32,128,128]{4,3,2,1,0:T(8,128)(2,1)}, u32[]{:S(2)}) %copy-start) | copy-done | bytes 1048600
  2.6 114.5 %shard_map.37 = f32[64,128,128]{2,1,0:T(8,128)S(1)} custom-call(s32[4,4,256]{2,1,0:T(4,128)S(1)} %pad_add_fusion.tables, bf16[32,128,128]{2,1,0:T(8,128)(2,1)S(1)} %bitcast.10, bf16[128,128,128]{2,1,0:T(8,128)(2,1)} %bitcast.14), custom_call_target="tpu_custom_call" | custom-call | flops 4294967296 | bytes 33554432 | tf_op jit(solution)/shard_map/pallas_call | solution.py:419
  117.1 2.0 %copy.12 = f32[1,1,64,128,128]{4,3,2,1,0:T(8,128)} copy(f32[1,1,64,128,128]{4,3,2,1,0:T(8,128)S(1)} %bitcast.9) | data formatting | bytes 8388608
  (8 shorter events, 0.1 us)
Async XLA Ops:
  1.4 1.2 %copy-start = (bf16[1,1,32,128,128]{4,3,2,1,0:T(8,128)(2,1)S(1)}, bf16[1,1,32,128,128]{4,3,2,1,0:T(8,128)(2,1)}, u32[]{:S(2)}) copy-start(bf16[1,1,32,128,128]{4,3,2,1,0:T(8,128)(2,1)} %param.3) | copy-start | bytes 3145732

commit v4 on v3

--- a/solution.py
+++ b/solution.py
@@ -246,6 +246,12 @@
         def _():
             lax.fori_loop(0, NC, send_one, 0)
 
+        @pl.when(at_start)
+        def _():
+            two.wait_recv()
+            products(a_two, b_own, tab_next, 0)
+            collect(part, tab_next, 0, False)
+
         def pass_on(k, carry):
             copy = remote(
                 b_chunk(b_prev, k), b_chunk(b_prev, k), b_send.at[k], b_recv.at[k], at(1, 0)
@@ -262,12 +268,17 @@
 
         far.wait_recv()
         products(a_even, b_prev, tab_next, 1)
-        collect(part, tab_next, 1, False)
-        two.wait_recv()
-        products(a_two, b_own, tab_next, 0)
+
+        @pl.when(jnp.logical_not(at_start))
+        def _():
+            collect(part, tab_next, 1, False)
+            two.wait_recv()
+            products(a_two, b_own, tab_next, 0)
+
+        own_step = jnp.where(at_start, 1, 0)
 
         def zero(k, carry):
-            encode_chunk(k, lambda c: part[c] + sums[tab_next[0, 3, c]], code_zero)
+            encode_chunk(k, lambda c: part[c] + sums[tab_next[own_step, 3, c]], code_zero)
             remote(code_zero.at[k], code_in.at[k], zero_send.at[k], c_recv.at[k], at(2, 0)).start()
             return carry
 
@@ -454,7 +465,7 @@
         cost_estimate=pl.CostEstimate(
             flops=2 * STEPS * NP * BS**3, bytes_accessed=32 << 20, transcendentals=0
         ),
-    )(tables, a, b)
+    )(tables, pltpu.with_memory_space_constraint(a, pltpu.HBM), b)
 
 
 def listed(pairs):

time: 119 us -> 118 us (level)
  local copies, waits for them, and re-layouts: 3.97 us -> 2.75 us
    unnamed x5 -> x3, local copies, waits for them, and re-layouts: 3.95 us -> 2.73 us
where the time goes in v4:
time: 118 us
  Pallas kernels  115 us (97%)
  local copies, waits for them, and re-layouts  2.75 us (2%)
    pallas_call x1, Pallas kernels, grid_product(): pl.pallas_call(kernel, out_shape=jax.ShapeDtypeStruct((CBLK, BS, BS), jnp...  115 us
    unnamed x3, local copies, waits for them, and re-layouts  2.73 us

profile of v4, /device:TPU:0, one launch (start us, length us, event | category | flops | bytes accessed | tf_op | source)
XLA Modules:
  0.0 118.2 jit_solution(14138992558130932799)
XLA Ops:
  0.0 0.7 copy.9
  0.8 0.5 select_reduce_fusion.1
  1.4 114.8 %shard_map.37 = f32[64,128,128]{2,1,0:T(8,128)S(1)} custom-call(s32[4,4,256]{2,1,0:T(4,128)S(1)} %pad_add_fusion.tables, bf16[32,128,128]{2,1,0:T(8,128)(2,1)} %bitcast.14, bf16[128,128,128]{2,1,0:T(8,128)(2,1)} %bitcast.13), custom_call_target="tpu_custom_call" | custom-call | flops 4294967296 | bytes 33554432 | tf_op jit(solution)/shard_map/pallas_call | solution.py:430
  116.2 2.0 %copy.12 = f32[1,1,64,128,128]{4,3,2,1,0:T(8,128)} copy(f32[1,1,64,128,128]{4,3,2,1,0:T(8,128)S(1)} %bitcast.9) | data formatting | bytes 8388608
  (8 shorter events, 0.1 us)
